TPU v7x, 256 devices: a whole 4x4x8 slice. The times are simulated.
256 devices in a mesh: snap: 16 (over z, core), vert: 16 (over y, x).
Axes of the slice: x: 4, y: 4, z: 8, core: 2. Of those that a mesh axis runs over, the one named last changes fastest.
Arguments:
- saved_gates: bfloat16 [16, 8192, 1536], P(None, ('vert', 'snap')), may hold values from -1 to 1, as said below
- saved_cells: bfloat16 [16, 8192, 384], P(None, ('vert', 'snap')), may hold values from -4 to 4
- conv_out: float32 [16, 8192, 384], P(None, ('vert', 'snap')), may hold values from -6 to 6
- out_grad: float32 [16, 8192, 384], P(None, ('vert', 'snap')), may hold values from -6 to 6
- input_weight: float32 [384, 1536], replicated, may hold values from -0.3125 to 0.3125
- recur_weight: float32 [384, 1536], replicated, may hold values from -0.3125 to 0.3125
- conv_weight: float32 [384, 384], replicated, may hold values from -0.3125 to 0.3125
- node_feats: float32 [16, 8192, 384], P('snap', 'vert'), may hold values from -6 to 6
- tile_values: bfloat16 [16, 16, 5, 512, 512], P('snap', 'vert'), may hold values from -0.15625 to 0.15625
- tile_mask: int32 [16, 16, 5], P('snap', 'vert'), may hold values 0 or 1
Outputs:
- feat_grad: float32 [16, 8192, 384], P('snap', 'vert')
- conv_weight_grad: float32 [147456], P(('snap', 'vert'))
- input_weight_grad: float32 [589824], P(('snap', 'vert'))
- recur_weight_grad: float32 [589824], P(('snap', 'vert'))
Inputs may be any that keep to these rules, and one draw needn't show every extreme that they name: `saved_gates`: the first and fourth blocks of 384 entries lie strictly between 0 and 1, the second in (0, 1], the third strictly between -1 and 1.
All inputs are finite; a program needn't handle non-finite values. No bound on the sum of `tile_mask` on one device may be relied on, other than what follows from the above.
Results may differ from a plain program's by a relative error of at most 0.0029.
Values may be sent and summed in bfloat16 or wider, within the bound.
A program may use at most 128 MiB of HBM per device.

v0:
```python
import jax
import jax.numpy as jnp
from jax import lax
from jax.sharding import PartitionSpec as P


def passed_along(shard, axis, by):
    size = lax.axis_size(axis)
    pairs = [(i, i + by) for i in range(size) if 0 <= i + by < size]
    return lax.ppermute(shard, axis, pairs)


def cell_backward(saved_gates, saved_cells, out_grad, recur_weight):
    feat_width = saved_cells.shape[-1]
    gate_vals = saved_gates.astype(jnp.float32)
    cell_vals = saved_cells.astype(jnp.float32)
    prev_cells = jnp.concatenate([jnp.zeros_like(cell_vals[:1]), cell_vals[:-1]], axis=0)

    def reverse_step(carry, inputs):
        rec_grad, cell_grad = carry
        gate_now, cell_now, cell_before, grad_now = inputs
        in_gate = gate_now[:, :feat_width]
        forget = gate_now[:, feat_width : 2 * feat_width]
        candidate = gate_now[:, 2 * feat_width : 3 * feat_width]
        out_gate = gate_now[:, 3 * feat_width :]
        total_grad = grad_now + rec_grad
        squashed = jnp.tanh(cell_now)
        cell_total = cell_grad + total_grad * out_gate * (1.0 - squashed * squashed)
        pre_grad = jnp.concatenate(
            [
                cell_total * candidate * in_gate * (1.0 - in_gate),
                cell_total * cell_before * forget * (1.0 - forget),
                cell_total * in_gate * (1.0 - candidate * candidate),
                total_grad * squashed * out_gate * (1.0 - out_gate),
            ],
            axis=-1,
        )
        new_rec = jnp.dot(
            pre_grad,
            recur_weight.T,
            precision=lax.Precision.HIGHEST,
            preferred_element_type=jnp.float32,
        )
        return ((new_rec, cell_total * forget), pre_grad)

    row_total = cell_vals.shape[1]
    begin = (
        jnp.zeros((row_total, feat_width), jnp.float32),
        jnp.zeros((row_total, feat_width), jnp.float32),
    )
    unused, pre_grads = lax.scan(
        reverse_step, begin, (gate_vals, cell_vals, prev_cells, out_grad), reverse=True
    )
    last_out = gate_vals[:, :, 3 * feat_width :]
    prev_out = jnp.concatenate([jnp.zeros_like(last_out[:1]), last_out[:-1]], axis=0)
    prev_hidden = prev_out * jnp.tanh(prev_cells)
    return (pre_grads, prev_hidden)


def pass_direct(piece, offset):
    return passed_along(piece, "vert", offset)


def local(
    saved_gates,
    saved_cells,
    conv_out,
    out_grad,
    input_weight,
    recur_weight,
    conv_weight,
    node_feats,
    tile_values,
    tile_mask,
):
    pre_grads, prev_hidden = cell_backward(saved_gates, saved_cells, out_grad, recur_weight)
    conv_in_grad = jnp.einsum(
        "tvg,fg->tvf",
        pre_grads,
        input_weight,
        precision=lax.Precision.HIGHEST,
        preferred_element_type=jnp.float32,
    )
    input_term = jnp.einsum(
        "tvf,tvg->fg",
        conv_out,
        pre_grads,
        precision=lax.Precision.HIGHEST,
        preferred_element_type=jnp.float32,
    ).reshape(-1)
    recur_term = jnp.einsum(
        "tvf,tvg->fg",
        prev_hidden,
        pre_grads,
        precision=lax.Precision.HIGHEST,
        preferred_element_type=jnp.float32,
    ).reshape(-1)
    input_weight_grad, recur_weight_grad = (
        lax.psum_scatter(input_term, ("snap", "vert"), scatter_dimension=0, tiled=True),
        lax.psum_scatter(recur_term, ("snap", "vert"), scatter_dimension=0, tiled=True),
    )
    rounded = lax.all_to_all(
        conv_in_grad.astype(jnp.bfloat16), "snap", split_axis=0, concat_axis=1, tiled=True
    )
    tiles = tile_values[:, 0]
    partial_value = jnp.einsum("skij,sif->skjf", tiles, rounded, preferred_element_type=jnp.float32)
    slot_count = tiles.shape[1]
    reach_blocks = (slot_count - 1) // 2
    position = lax.axis_index("vert")
    block_count = lax.axis_size("vert")
    target = position + jnp.arange(slot_count, dtype=jnp.int32) - reach_blocks
    inside = (target >= 0) & (target < block_count)
    present = (tile_mask[:, 0, :] == 1) & inside[None, :]
    partial_value = partial_value * present.astype(jnp.float32)[:, :, None, None]
    z_grad = partial_value[:, reach_blocks]
    for slot in range(slot_count):
        offset = slot - reach_blocks
        if offset != 0:
            z_grad = z_grad + pass_direct(partial_value[:, slot], offset)
    feat_grad = jnp.einsum(
        "sbg,fg->sbf",
        z_grad,
        conv_weight,
        precision=lax.Precision.HIGHEST,
        preferred_element_type=jnp.float32,
    )
    conv_term = jnp.einsum(
        "sbf,sbg->fg",
        node_feats,
        z_grad,
        precision=lax.Precision.HIGHEST,
        preferred_element_type=jnp.float32,
    ).reshape(-1)
    conv_weight_grad = lax.psum_scatter(
        conv_term, ("snap", "vert"), scatter_dimension=0, tiled=True
    )
    return (feat_grad, conv_weight_grad, input_weight_grad, recur_weight_grad)


def solution(mesh):
    placed = (
        P(None, ("vert", "snap"), None),
        P(None, ("vert", "snap"), None),
        P(None, ("vert", "snap"), None),
        P(None, ("vert", "snap"), None),
        P(),
        P(),
        P(),
        P("snap", "vert", None),
        P("snap", "vert", None, None, None),
        P("snap", "vert", None),
    )
    return jax.shard_map(
        local,
        mesh=mesh,
        in_specs=placed,
        out_specs=(
            P("snap", "vert", None),
            P(("snap", "vert")),
            P(("snap", "vert")),
            P(("snap", "vert")),
        ),
        check_vma=False,
    )
```

profile of v0, /device:TPU:8, one launch (start us, length us, event | category | flops | bytes accessed | tf_op | source)
XLA Modules:
  0.0 538.3 jit_solution(3331778018956491245)
XLA Ops:
  8.4 2.0 convert_element_type.19
  10.4 3.5 convert_element_type.18
  14.8 2.1 broadcast_in_dim.15
  17.5 135.6 %while.19 = (s32[]{:T(128)}, f32[32,384]{1,0:T(8,128)}, f32[32,384]{1,0:T(8,128)}, f32[16,32,1536]{2,1,0:T(8,128)}, f32[16,32,384]{2,1,0:T(8,128)}, /*index=5*/f...) while((s32[]{:T(128)}, f32[32,384]{1,0:T(8,128)}, ...), condition=%wide.region_1.2_spmd.clone, body=%wide.region_0.1_spmd.clone.sunk | while | flops 227082240 | bytes 4227227 | solution.py:51
  21.5 4.5 fusion.44
  29.9 4.5 fusion.44
  35.4 1.5 slice_multiply_fusion.2
  38.4 4.5 fusion.44
  46.9 4.5 fusion.44
  55.3 4.5 fusion.44
  63.8 4.5 fusion.44
  72.3 4.5 fusion.44
  80.8 4.5 fusion.44
  89.3 4.5 fusion.44
  94.7 1.5 slice_multiply_fusion.2
  97.8 4.5 fusion.44
  106.2 4.5 fusion.44
  111.7 1.5 slice_multiply_fusion.2
  114.7 4.5 fusion.44
  123.2 4.5 fusion.44
  131.7 4.5 fusion.44
  137.1 1.5 slice_multiply_fusion.2
  140.2 4.5 fusion.44
  148.6 4.5 fusion.44
  153.1 8.5 %fusion.15 = bf16[16,32,384]{2,1,0:T(8,128)(2,1)} fusion(f32[16,32,1536]{2,1,0:T(8,128)} %get-tuple-element.183, f32[384,1536]{1,0:T(8,128)} %param.16), kind=kOutput, calls=%fused_computation.28 | convolution fusion | flops 3624075264 | bytes 5898240 | tf_op jit(solution)/shard_map/tvg,fg->tvf/dot_general | solution.py:77
  161.6 8.6 %all-to-all-start = ((bf16[16,32,384]{2,1,0:T(8,128)(2,1)}), bf16[16,32,384]{2,1,0:T(8,128)(2,1)}, u32[]{:S(2)}, u32[]{:S(2)}) async-start(bf16[16,32,384]{2,1,0:T(8,128)(2,1)} %fusion.15), calls=%async_computation | async-start | bytes 786432 | tf_op jit(solution)/shard_map/all_to_all | solution.py:102
  170.3 1.9 slice.80
  172.2 11.8 %all-to-all-done = bf16[16,32,384]{2,1,0:T(8,128)(2,1)} async-done(((bf16[16,32,384]{2,1,0:T(8,128)(2,1)}), bf16[16,32,384]{2,1,0:T(8,128)(2,1)}, u32[]{:S(2)}, u32[]{:S(2)}) %all-to-all-start) | async-done | bytes 393248 | tf_op jit(solution)/shard_map/all_to_all | solution.py:102
  184.0 2.2 multiply_bitcast_fusion
  186.2 1.7 slice_bitcast_fusion.3
  187.9 1.8 copy-done.1
  189.7 4.9 collective-permute-start
  194.6 3.1 collective-permute-start.1
  197.7 2.8 collective-permute-start.2
  200.5 2.6 collective-permute-start.3
  203.1 5.4 %convolution_bitcast_fusion = f32[384,1536]{1,0:T(8,128)} fusion(f32[16,32,1536]{2,1,0:T(8,128)S(1)} %copy-done.2, f32[15,32,384]{2,1,0:T(8,128)S(1)} %copy-done.4, f32[15,32,384]{2,1,0:T(8,128)S(1)} %slice.74), kind=kOutput, calls=%fused_computation.21 | convolution fusion | flops 3624075264 | bytes 6979584 | tf_op jit(solution)/shard_map/tvf,tvg->fg/dot_general | solution.py:91
  208.6 3.2 reshape.70
  211.8 7.7 %convolution_bitcast_fusion.1 = f32[384,1536]{0,1:T(8,128)} fusion(f32[16,32,1536]{2,1,0:T(8,128)} %get-tuple-element.183, f32[16,32,384]{2,1,0:T(8,128)S(1)} %copy-done.5), kind=kOutput, calls=%fused_computation.22 | convolution fusion | flops 3623878656 | bytes 6291456 | tf_op jit(solution)/shard_map/tvf,tvg->fg/dot_general | solution.py:84
  219.5 3.1 copy.20
  222.6 3.1 reshape.69
  225.8 4.8 collective-permute-done.1
  230.9 16.3 %collective-permute-done.3 = f32[1,512,384]{1,2,0:T(8,128)} collective-permute-done((f32[1,512,384]{1,2,0:T(8,128)}, f32[1,512,384]{1,2,0:T(8,128)}, u32[]{:S(2)}, u32[]{:S(2)}) %collective-permute-start.3) | collective-permute-done | bytes 786464 | tf_op jit(solution)/shard_map/ppermute | solution.py:10
  247.3 2.5 fusion.22
  249.8 2.2 convolution_bitcast_fusion.3
  252.0 2.1 copy.19
  254.2 1.9 reshape.68
  256.1 4.6 convolution_bitcast_fusion.2
  260.7 266.6 %all-reduce.8.cloned.1.call-done = (f32[147456]{0:T(1024)}, f32[589824]{0:T(1024)}, f32[589824]{0:T(1024)}) async-done(((f32[147456]{0:T(1024)}, f32[589824]{0:T(1024)}, f32[589824]{0:T(1024)}), (f32[147456]{0:T(1024)}, f32[589824]{0:T(1024)}, f32[589824]{0:T(1024)})) %all-reduce.8.cloned.1.call-update) | async-done | bytes 5308432
  (85 shorter events, 65.2 us)
Async XLA Ops:
  7.2 176.8 %copy-start = (bf16[1,1,5,512,512]{4,3,2,1,0:T(8,128)(2,1)S(1)}, bf16[1,1,5,512,512]{4,3,2,1,0:T(8,128)(2,1)}, u32[]{:S(2)}) copy-start(bf16[1,1,5,512,512]{4,3,2,1,0:T(8,128)(2,1)} %param.20) | copy-start | bytes 7864324
  153.1 19.1 %copy-start.6 = (s32[1,1,5]{2,1,0:T(1,128)S(1)}, s32[1,1,5]{2,1,0:T(1,128)}, u32[]{:S(2)}) copy-start(s32[1,1,5]{2,1,0:T(1,128)} %param.21) | copy-start | bytes 64
  161.6 22.4 %all-to-all-start = ((bf16[16,32,384]{2,1,0:T(8,128)(2,1)}), bf16[16,32,384]{2,1,0:T(8,128)(2,1)}, u32[]{:S(2)}, u32[]{:S(2)}) async-start(bf16[16,32,384]{2,1,0:T(8,128)(2,1)} %fusion.15), calls=%async_computation | async-start | bytes 786432 | tf_op jit(solution)/shard_map/all_to_all | solution.py:102
  170.2 357.1 %all-reduce.8.cloned.1.call-start = ((), (), s32[]{:S(2)}) async-start(), calls=%async_computation.1 | async-start | bytes 10616832
  186.2 3.5 copy-start.1
  186.2 16.9 %copy-start.2 = (f32[16,32,1536]{2,1,0:T(8,128)S(1)}, f32[16,32,1536]{2,1,0:T(8,128)}, u32[]{:S(2)}) copy-start(f32[16,32,1536]{2,1,0:T(8,128)} %get-tuple-element.183) | copy-start | bytes 9437188
  186.2 16.9 %copy-start.4 = (f32[15,32,384]{2,1,0:T(8,128)S(1)}, f32[15,32,384]{2,1,0:T(8,128)}, u32[]{:S(2)}) copy-start(f32[15,32,384]{2,1,0:T(8,128)} %slice.80) | copy-start | bytes 2211844
  189.7 36.1 %collective-permute-start = (f32[1,512,384]{1,2,0:T(8,128)}, f32[1,512,384]{1,2,0:T(8,128)}, u32[]{:S(2)}, u32[]{:S(2)}) collective-permute-start(f32[1,512,384]{1,2,0:T(8,128)} %get-tuple-element.241), channel_id=1, source_target_pairs={{2,0},{3,1},{4,2},{5,3},{6,4},{7,5},{8,6},{9,7},{10,8},{11,9},{12,... | collective-permute-start | bytes 2359304 | tf_op jit(solution)/shard_map/ppermute | solution.py:10
  194.6 35.9 %collective-permute-start.1 = (f32[1,512,384]{1,2,0:T(8,128)}, f32[1,512,384]{1,2,0:T(8,128)}, u32[]{:S(2)}, u32[]{:S(2)}) collective-permute-start(f32[1,512,384]{1,2,0:T(8,128)} %get-tuple-element.244), channel_id=1, source_target_pairs={{1,0},{2,1},{3,2},{4,3},{5,4},{6,5},{7,6},{8,7},{9,8},{10,9},{11,1... | collective-permute-start | bytes 2359304 | tf_op jit(solution)/shard_map/ppermute | solution.py:10
  197.7 33.2 %collective-permute-start.2 = (f32[1,512,384]{1,2,0:T(8,128)}, f32[1,512,384]{1,2,0:T(8,128)}, u32[]{:S(2)}, u32[]{:S(2)}) collective-permute-start(f32[1,512,384]{1,2,0:T(8,128)} %get-tuple-element.243), channel_id=1, source_target_pairs={{0,1},{1,2},{2,3},{3,4},{4,5},{5,6},{6,7},{7,8},{8,9},{9,10},{10,1... | collective-permute-start | bytes 2359304 | tf_op jit(solution)/shard_map/ppermute | solution.py:10
  200.5 46.8 %collective-permute-start.3 = (f32[1,512,384]{1,2,0:T(8,128)}, f32[1,512,384]{1,2,0:T(8,128)}, u32[]{:S(2)}, u32[]{:S(2)}) collective-permute-start(f32[1,512,384]{1,2,0:T(8,128)} %get-tuple-element.242), channel_id=1, source_target_pairs={{0,2},{1,3},{2,4},{3,5},{4,6},{5,7},{6,8},{7,9},{8,10},{9,11},{10,... | collective-permute-start | bytes 2359304 | tf_op jit(solution)/shard_map/ppermute | solution.py:10
  208.6 3.2 copy-start.5
  225.8 24.1 %copy-start.3 = (f32[1,512,384]{2,1,0:T(8,128)S(1)}, f32[1,512,384]{2,1,0:T(8,128)}, u32[]{:S(2)}) copy-start(f32[1,512,384]{2,1,0:T(8,128)} %param.19) | copy-start | bytes 2359300
Sparse Core Ops, SparseCore 0:
  256.2 271.0 all-reduce.7
where the time goes:
time: 542 us; the launch traced here: 538 us
  waiting for transfers between devices  300 us (55%)
  matrix products  102 us (19%)
  other arithmetic  56.7 us (10%)
  local copies, waits for them, and re-layouts  43 us (8%)
  starting transfers between devices  22.1 us (4%)
  between operations  14.2 us (3%)
    unnamed x2, waiting for transfers between devices  267 us
    dot_general x16, matrix products, reverse_step(): jnp.dot(pre_grad, recur_weight.T, precision=lax.Precision.HIGHEST, prefer...  71.7 us
    mul x16, other arithmetic, reverse_step(): return ((new_rec, cell_total * forget), pre_grad)  24.4 us
    ppermute x4, waiting for transfers between devices, passed_along(): return lax.ppermute(shard, axis, pairs)  21.5 us
    squeeze x16, local copies, waits for them, and re-layouts, cell_backward(): lax.scan(reverse_step, begin, (gate_vals, cell_vals, prev_cells, out_grad...  15 us
    ppermute x4, starting transfers between devices, passed_along(): return lax.ppermute(shard, axis, pairs)  13.4 us
    mul x16, other arithmetic, reverse_step(): cell_total * candidate * in_gate * (1.0 - in_gate)  13.2 us
    all_to_all x1, waiting for transfers between devices, local(): lax.all_to_all(conv_in_grad.astype(jnp.bfloat16), 'snap', split_axis=0, c...  11.8 us
  transfers between devices with their start and end apart: 6, of which 5 were waited for; matrix products, arithmetic and copies ran while one was open for 5% of the time, Pallas kernels for 0%

commit v1 on v0

v1 whole, which is shorter than its diff:
```python
import jax
import jax.numpy as jnp
from jax import lax
from jax.experimental import pallas as pl
from jax.experimental.pallas import tpu as pltpu
from jax.sharding import PartitionSpec as P

F32, BF16 = jnp.float32, jnp.bfloat16
VMEM_CAP = 60 * 1024 * 1024


def split_store(value, hi_ref, lo_ref):
    high = value.astype(BF16)
    hi_ref[...] = high
    lo_ref[...] = (value - high.astype(F32)).astype(BF16)


def dot3(a_hi, a_lo, b_hi, b_lo, dims):
    one = lambda a, b: lax.dot_general(a, b, (dims, ((), ())), preferred_element_type=F32)
    return one(a_hi, b_hi) + (one(a_lo, b_hi) + one(a_hi, b_lo))


def scan_kernel(
    gates, cells, grads, recur_t, input_t,
    rounded, pre_hi, pre_lo, hid_hi, hid_lo,
    r_hi, r_lo, i_hi, i_lo, rec, cell_grad,
):
    steps, rows, feat = cells.shape
    split_store(recur_t[...], r_hi, r_lo)
    split_store(input_t[...], i_hi, i_lo)
    rec[...] = jnp.zeros_like(rec)
    cell_grad[...] = jnp.zeros_like(cell_grad)
    two = ((1,), (0,))

    def step(n, carry):
        t = steps - 1 - n
        before = jnp.maximum(t - 1, 0)
        live = (t > 0).astype(F32)
        part = lambda k: gates[t, :, k * feat : (k + 1) * feat].astype(F32)
        in_gate, forget, candidate, out_gate = part(0), part(1), part(2), part(3)
        squashed = jnp.tanh(cells[t].astype(F32))
        cell_before = cells[before].astype(F32) * live
        hidden = gates[before, :, 3 * feat :].astype(F32) * jnp.tanh(cell_before)
        high = hidden.astype(BF16)
        hid_hi[t] = high
        hid_lo[t] = (hidden - high.astype(F32)).astype(BF16)
        total = grads[t] + rec[...]
        cell_total = cell_grad[...] + total * (out_gate * (1.0 - squashed * squashed))
        pieces = [
            cell_total * (candidate * in_gate * (1.0 - in_gate)),
            cell_total * (cell_before * forget * (1.0 - forget)),
            cell_total * (in_gate * (1.0 - candidate * candidate)),
            total * (squashed * out_gate * (1.0 - out_gate)),
        ]
        cell_grad[...] = cell_total * forget
        acc = None
        for k, piece in enumerate(pieces):
            cols = slice(k * feat, (k + 1) * feat)
            high = piece.astype(BF16)
            low = (piece - high.astype(F32)).astype(BF16)
            pre_hi[t, :, cols] = high
            pre_lo[t, :, cols] = low
            both = jnp.concatenate([high, low], axis=0)
            main = jnp.dot(both, r_hi[cols, :], preferred_element_type=F32)
            side = jnp.dot(high, r_lo[cols, :], preferred_element_type=F32)
            term = main[:rows] + (main[rows:] + side)
            acc = term if acc is None else acc + term
        rec[...] = acc
        return carry

    lax.fori_loop(0, steps, step, 0)
    group = 4

    def project(n, carry):
        at = pl.ds(n * group, group)
        shape = (group * rows, 4 * feat)
        value = dot3(
            pre_hi[at].reshape(shape), pre_lo[at].reshape(shape), i_hi[...], i_lo[...], two
        )
        rounded[at] = value.astype(BF16).reshape(group, rows, feat)
        return carry

    lax.fori_loop(0, steps // group, project, 0)


def run_scan(gates, cells, grads, recur_t, input_t):
    steps, rows, feat = cells.shape
    wide = 4 * feat
    vm = pl.BlockSpec(memory_space=pltpu.VMEM)
    shape = lambda *s: jax.ShapeDtypeStruct(s, BF16)
    return pl.pallas_call(
        scan_kernel,
        in_specs=[vm] * 5,
        out_specs=[vm] * 5,
        out_shape=[
            shape(steps, rows, feat), shape(steps, rows, wide), shape(steps, rows, wide),
            shape(steps, rows, feat), shape(steps, rows, feat),
        ],
        scratch_shapes=[
            pltpu.VMEM((wide, feat), BF16), pltpu.VMEM((wide, feat), BF16),
            pltpu.VMEM((wide, feat), BF16), pltpu.VMEM((wide, feat), BF16),
            pltpu.VMEM((rows, feat), F32), pltpu.VMEM((rows, feat), F32),
        ],
        compiler_params=pltpu.CompilerParams(vmem_limit_bytes=VMEM_CAP),
        name="scan",
    )(gates, cells, grads, recur_t, input_t)


def weight_kernel(conv_out, hid_hi, hid_lo, pre_hi, pre_lo, out, c_hi, c_lo):
    rows, feat = conv_out.shape
    wide = pre_hi.shape[1]
    split_store(conv_out[...], c_hi, c_lo)
    first = ((0,), (0,))
    width = 512

    def block(n, carry):
        at = pl.ds(pl.multiple_of(n * width, width), width)
        p_hi, p_lo = pre_hi[:, at], pre_lo[:, at]
        out[0, :, at] = dot3(c_hi[...], c_lo[...], p_hi, p_lo, first).astype(out.dtype)
        out[1, :, at] = dot3(hid_hi[...], hid_lo[...], p_hi, p_lo, first).astype(out.dtype)
        return carry

    lax.fori_loop(0, wide // width, block, 0)


def run_weights(conv_out, hid_hi, hid_lo, pre_hi, pre_lo):
    rows, feat = conv_out.shape
    wide = pre_hi.shape[1]
    vm = pl.BlockSpec(memory_space=pltpu.VMEM)
    flops = 12 * rows * feat * wide
    return pl.pallas_call(
        weight_kernel,
        in_specs=[vm] * 5,
        out_specs=vm,
        out_shape=jax.ShapeDtypeStruct((2, feat, wide), BF16),
        scratch_shapes=[pltpu.VMEM((rows, feat), BF16), pltpu.VMEM((rows, feat), BF16)],
        compiler_params=pltpu.CompilerParams(vmem_limit_bytes=VMEM_CAP),
        cost_estimate=pl.CostEstimate(flops=flops, bytes_accessed=8 << 20, transcendentals=0),
        name="weights",
    )(conv_out, hid_hi, hid_lo, pre_hi, pre_lo)


def tile_kernel(present, tiles, rounded, away, home):
    slots = tiles.shape[0]
    reach = slots // 2
    at = 0
    for slot in range(slots):
        keep = present[slot].astype(F32)
        value = lax.dot_general(
            tiles[slot], rounded[...], (((0,), (0,)), ((), ())), preferred_element_type=F32
        ) * keep
        if slot == reach:
            home[...] = value
        else:
            away[at] = value.astype(BF16)
            at += 1


def run_tiles(present, tiles, rounded):
    slots, block, _ = tiles.shape
    feat = rounded.shape[1]
    vm = pl.BlockSpec(memory_space=pltpu.VMEM)
    return pl.pallas_call(
        tile_kernel,
        in_specs=[pl.BlockSpec(memory_space=pltpu.SMEM), vm, vm],
        out_specs=[vm, vm],
        out_shape=[
            jax.ShapeDtypeStruct((slots - 1, block, feat), BF16),
            jax.ShapeDtypeStruct((block, feat), F32),
        ],
        compiler_params=pltpu.CompilerParams(vmem_limit_bytes=VMEM_CAP),
        name="tiles",
    )(present, tiles, rounded)


def passed_along(shard, axis, by):
    size = lax.axis_size(axis)
    pairs = [(i, i + by) for i in range(size) if 0 <= i + by < size]
    return lax.ppermute(shard, axis, pairs)


def summed_pieces(pieces, axis):
    got = lax.all_to_all(pieces, axis, split_axis=0, concat_axis=0, tiled=True)
    return jnp.sum(got.astype(F32), axis=0)


def local(
    saved_gates, saved_cells, conv_out, out_grad, input_weight, recur_weight,
    conv_weight, node_feats, tile_values, tile_mask,
):
    steps, rows, feat = saved_cells.shape
    wide = 4 * feat
    snaps, blocks = lax.axis_size("snap"), lax.axis_size("vert")
    rounded, pre_hi, pre_lo, hid_hi, hid_lo = run_scan(
        saved_gates, saved_cells, out_grad, recur_weight.T, input_weight.T
    )
    arrived = lax.all_to_all(rounded, "snap", split_axis=0, concat_axis=1, tiled=True)
    flat = lambda a: a.reshape(steps * rows, a.shape[-1])
    terms = run_weights(flat(conv_out), flat(hid_hi), flat(hid_lo), flat(pre_hi), flat(pre_lo))
    own = feat // snaps
    terms = terms.reshape(2, snaps, own, wide).transpose(1, 0, 2, 3)

    tiles = tile_values[0, 0]
    slot_count = tiles.shape[0]
    reach = slot_count // 2
    target = lax.axis_index("vert") + jnp.arange(slot_count, dtype=jnp.int32) - reach
    inside = (target >= 0) & (target < blocks)
    present = ((tile_mask[0, 0] == 1) & inside).astype(jnp.int32)
    away, z_grad = run_tiles(present, tiles, arrived[0])
    offsets = [k - reach for k in range(slot_count) if k != reach]
    moved = [passed_along(away[n], "vert", by) for n, by in enumerate(offsets)]
    for part in moved:
        z_grad = z_grad + part.astype(F32)
    feat_grad = jnp.einsum(
        "bg,fg->bf", z_grad, conv_weight, precision=lax.Precision.HIGH, preferred_element_type=F32
    )[None]
    conv_term = jnp.einsum(
        "bf,bg->fg", node_feats[0], z_grad, precision=lax.Precision.HIGH, preferred_element_type=F32
    )
    first = summed_pieces(terms, "snap")
    lstm = first.reshape(2, blocks, own * wide // blocks).transpose(1, 0, 2)
    lstm = summed_pieces(lstm, "vert")
    conv = summed_pieces(conv_term.reshape(snaps, own, feat).astype(BF16), "snap")
    conv = summed_pieces(conv.reshape(blocks, own * feat // blocks), "vert")
    return (feat_grad, conv, lstm[0], lstm[1])


def solution(mesh):
    along = P(None, ("vert", "snap"), None)
    placed = (
        along, along, along, along, P(), P(), P(),
        P("snap", "vert", None), P("snap", "vert", None, None, None), P("snap", "vert", None),
    )
    both = P(("snap", "vert"))
    return jax.shard_map(
        local,
        mesh=mesh,
        in_specs=placed,
        out_specs=(P("snap", "vert", None), both, both, both),
        check_vma=False,
    )
```

time: 542 us -> 190 us (0.35)
  waiting for transfers between devices: 300 us -> 89.5 us
  matrix products: 102 us -> 5.16 us
  other arithmetic: 56.7 us -> 4.68 us
  Pallas kernels: 0 us -> 28.7 us
  local copies, waits for them, and re-layouts: 43 us -> 15.7 us
  starting transfers between devices: 22.1 us -> 44.3 us
  between operations: 14.2 us -> 0.75 us
    unnamed x2 -> x0, waiting for transfers between devices: 267 us -> none
    dot_general x22 -> x2, matrix products: 102 us -> 5.16 us  [the longest x1 3.49 us: local(): jnp.einsum('bg,fg->bf', z_grad, conv_weight, precision=lax.Precision.HIGH...]
    all_to_all x1 -> x5, waiting for transfers between devices: 11.8 us -> 70.6 us  [the longest x4 57.4 us: summed_pieces(): got = lax.all_to_all(pieces, axis, split_axis=0, concat_axis=0, tiled=True)]
    mul x32 -> x0, other arithmetic: 37.5 us -> none  [the longest x16 24.4 us: reverse_step(): return ((new_rec, cell_total * forget), pre_grad)]
    pallas_call x0 -> x3, Pallas kernels: none -> 28.7 us  [the longest x1 16.1 us: run_scan(): pl.pallas_call(scan_kernel, in_specs=[vm] * 5, out_specs=[vm] * 5, out_sh...]
    all_to_all x1 -> x5, starting transfers between devices: 8.62 us -> 31 us  [the longest x4 22.5 us: summed_pieces(): got = lax.all_to_all(pieces, axis, split_axis=0, concat_axis=0, tiled=True)]
    squeeze x17 -> x1, local copies, waits for them, and re-layouts: 16.7 us -> 1.58 us  [local(): moved = [passed_along(away[n], 'vert', by) for n, by in enumerate(offsets)]]
    dynamic_update_slice x16 -> x0, other arithmetic: 11.2 us -> none  [cell_backward(): lax.scan(reverse_step, begin, (gate_vals, cell_vals, prev_cells, out_grad...]
  transfers between devices with their start and end apart: 6 -> 9, of which waited for: 5 -> 8; matrix products, arithmetic and copies ran while one was open for 5% -> 7% of each run, Pallas kernels for 0% -> 4%
where the time goes in v1:
time: 190 us; the launch traced here: 189 us
  waiting for transfers between devices  89.5 us (47%)
  starting transfers between devices  44.3 us (23%)
  Pallas kernels  28.7 us (15%)
  local copies, waits for them, and re-layouts  15.7 us (8%)
  matrix products  5.16 us (3%)
  other arithmetic  4.68 us (2%)
    all_to_all x4, waiting for transfers between devices, summed_pieces(): got = lax.all_to_all(pieces, axis, split_axis=0, concat_axis=0, tiled=True)  57.4 us
    all_to_all x4, starting transfers between devices, summed_pieces(): got = lax.all_to_all(pieces, axis, split_axis=0, concat_axis=0, tiled=True)  22.5 us
    ppermute x4, waiting for transfers between devices, passed_along(): return lax.ppermute(shard, axis, pairs)  18.9 us
    pallas_call x1, Pallas kernels, run_scan(): pl.pallas_call(scan_kernel, in_specs=[vm] * 5, out_specs=[vm] * 5, out_sh...  16.1 us
    ppermute x4, starting transfers between devices, passed_along(): return lax.ppermute(shard, axis, pairs)  13.3 us
    all_to_all x1, waiting for transfers between devices, local(): lax.all_to_all(rounded, 'snap', split_axis=0, concat_axis=1, tiled=True)  13.2 us
    all_to_all x1, starting transfers between devices, local(): lax.all_to_all(rounded, 'snap', split_axis=0, concat_axis=1, tiled=True)  8.57 us
    pallas_call x1, Pallas kernels, run_weights(): pl.pallas_call(weight_kernel, in_specs=[vm] * 5, out_specs=vm, out_shape=...  8.13 us
  transfers between devices with their start and end apart: 9, of which 8 were waited for; matrix products, arithmetic and copies ran while one was open for 7% of the time, Pallas kernels for 4%

profile of v1, /device:TPU:8, one launch (start us, length us, event | category | flops | bytes accessed | tf_op | source)
XLA Modules:
  0.0 188.8 jit_solution(15044601261742960731)
XLA Ops:
  0.6 0.0 copy-start
  0.6 0.0 copy-start.2
  0.7 3.2 %copy.19 = f32[384,1536]{0,1:T(8,128)} copy(f32[384,1536]{1,0:T(8,128)} %param.15) | data formatting | bytes 4718592 | tf_op args[5]
  3.9 0.0 copy-done.2
  3.9 2.0 %copy.20 = f32[384,1536]{0,1:T(8,128)} copy(f32[384,1536]{1,0:T(8,128)S(1)} %copy-done.2) | data formatting | bytes 4718592 | tf_op args[4]
  5.8 0.0 copy-start.8
  5.8 16.1 %scan.1 = (bf16[16,32,384]{2,1,0:T(8,128)(2,1)}, bf16[16,32,1536]{2,1,0:T(8,128)(2,1)}, bf16[16,32,1536]{2,1,0:T(8,128)(2,1)}, bf16[16,32,384]{2,1,0:T(8,128)(2,1)}, bf16[16,32,384]{2,1,0:T(8,128)(2,1)}) custom-call(bf16[16,32,1536]{2,1,0:T(8,128)(2,1)} %gates.1, bf16[16,32,384]{2,1,0:T(8,128)(2,1)} %cells.1, f32[16,32,384]{2,1,0:T(8,128)} %grads.1, ...), custom_call_target="tpu_custom_call" | custom-call | tf_op jit(solution)/shard_map/scan/pallas_call | solution.py:91
  21.9 8.6 %all-to-all-start = ((bf16[16,32,384]{2,1,0:T(8,128)(2,1)}), bf16[16,32,384]{2,1,0:T(8,128)(2,1)S(1)}, u32[]{:S(2)}, u32[]{:S(2)}) async-start(bf16[16,32,384]{2,1,0:T(8,128)(2,1)} %get-tuple-element.11), calls=%async_computation | async-start | bytes 786432 | tf_op jit(solution)/shard_map/all_to_all | solution.py:197
  30.5 0.0 copy-done.8
  30.5 0.5 fusion.1.present
  31.1 13.2 %all-to-all-done = bf16[16,32,384]{2,1,0:T(8,128)(2,1)S(1)} async-done(((bf16[16,32,384]{2,1,0:T(8,128)(2,1)}), bf16[16,32,384]{2,1,0:T(8,128)(2,1)S(1)}, u32[]{:S(2)}, u32[]{:S(2)}) %all-to-all-start) | async-done | bytes 393248 | tf_op jit(solution)/shard_map/all_to_all | solution.py:197
  44.2 0.7 copy-done.3
  45.0 4.5 %tiles.1 = (bf16[4,512,384]{2,1,0:T(8,128)(2,1)}, f32[512,384]{1,0:T(8,128)}) custom-call(s32[5]{0:T(128)} %fusion.1.present, bf16[5,512,512]{2,1,0:T(8,128)(2,1)} %bitcast.38, bf16[512,384]{1,0:T(8,128)(2,1)} %bitcast.40), custom_call_target="tpu_custom_call" | custom-call | tf_op jit(solution)/shard_map/tiles/pallas_call | solution.py:163
  49.5 1.6 slice_bitcast_fusion.3
  51.0 4.8 %collective-permute-start = (bf16[512,384]{1,0:T(8,128)(2,1)S(1)}, bf16[512,384]{1,0:T(8,128)(2,1)S(1)}, u32[]{:S(2)}, u32[]{:S(2)}) collective-permute-start(bf16[512,384]{1,0:T(8,128)(2,1)S(1)} %get-tuple-element.20), channel_id=1, source_target_pairs={{2,0},{3,1},{4,2},{5,3},{6,4},{7,5},{8,6},{9,7},{10,8},{11,9},{12,... | collective-permute-start | bytes 1179656 | tf_op jit(solution)/shard_map/ppermute | solution.py:179
  55.9 3.0 %collective-permute-start.1 = (bf16[512,384]{1,0:T(8,128)(2,1)S(1)}, bf16[512,384]{1,0:T(8,128)(2,1)S(1)}, u32[]{:S(2)}, u32[]{:S(2)}) collective-permute-start(bf16[512,384]{1,0:T(8,128)(2,1)S(1)} %get-tuple-element.23), channel_id=1, source_target_pairs={{1,0},{2,1},{3,2},{4,3},{5,4},{6,5},{7,6},{8,7},{9,8},{10,9},{11,1... | collective-permute-start | bytes 1179656 | tf_op jit(solution)/shard_map/ppermute | solution.py:179
  58.9 2.8 %collective-permute-start.2 = (bf16[512,384]{1,0:T(8,128)(2,1)S(1)}, bf16[512,384]{1,0:T(8,128)(2,1)S(1)}, u32[]{:S(2)}, u32[]{:S(2)}) collective-permute-start(bf16[512,384]{1,0:T(8,128)(2,1)S(1)} %get-tuple-element.22), channel_id=1, source_target_pairs={{0,1},{1,2},{2,3},{3,4},{4,5},{5,6},{6,7},{7,8},{8,9},{9,10},{10,1... | collective-permute-start | bytes 1179656 | tf_op jit(solution)/shard_map/ppermute | solution.py:179
  61.7 2.6 %collective-permute-start.3 = (bf16[512,384]{1,0:T(8,128)(2,1)S(1)}, bf16[512,384]{1,0:T(8,128)(2,1)S(1)}, u32[]{:S(2)}, u32[]{:S(2)}) collective-permute-start(bf16[512,384]{1,0:T(8,128)(2,1)S(1)} %get-tuple-element.21), channel_id=1, source_target_pairs={{0,2},{1,3},{2,4},{3,5},{4,6},{5,7},{6,8},{7,9},{8,10},{9,11},{10,... | collective-permute-start | bytes 1179656 | tf_op jit(solution)/shard_map/ppermute | solution.py:179
  64.4 1.8 collective-permute-done
  66.1 8.4 %collective-permute-done.1 = bf16[512,384]{1,0:T(8,128)(2,1)S(1)} collective-permute-done((bf16[512,384]{1,0:T(8,128)(2,1)S(1)}, bf16[512,384]{1,0:T(8,128)(2,1)S(1)}, u32[]{:S(2)}, u32[]{:S(2)}) %collective-permute-start.1) | collective-permute-done | bytes 393248 | tf_op jit(solution)/shard_map/ppermute | solution.py:179
  74.6 8.7 %collective-permute-done.2 = bf16[512,384]{1,0:T(8,128)(2,1)S(1)} collective-permute-done((bf16[512,384]{1,0:T(8,128)(2,1)S(1)}, bf16[512,384]{1,0:T(8,128)(2,1)S(1)}, u32[]{:S(2)}, u32[]{:S(2)}) %collective-permute-start.2) | collective-permute-done | bytes 393248 | tf_op jit(solution)/shard_map/ppermute | solution.py:179
  83.3 0.0 collective-permute-done.3
  83.3 0.0 copy-done
  83.3 0.0 copy-done.1
  83.3 1.7 convolution_convert_fusion
  85.0 0.0 copy-done.4
  85.0 0.0 copy-done.5
  85.0 0.0 copy-done.6
  85.0 3.5 %all-to-all-start.1 = ((bf16[16,24,384]{2,1,0:T(8,128)(2,1)}), bf16[16,24,384]{2,1,0:T(8,128)(2,1)S(1)}, u32[]{:S(2)}, u32[]{:S(2)}) async-start(bf16[16,24,384]{2,1,0:T(8,128)(2,1)} %bitcast.12), calls=%async_computation.1 | async-start | bytes 589824 | tf_op jit(solution)/shard_map/all_to_all | solution.py:183
  88.5 8.1 %weights.1 = bf16[2,384,1536]{2,1,0:T(8,128)(2,1)} custom-call(f32[512,384]{1,0:T(8,128)} %bitcast.44, bf16[512,384]{1,0:T(8,128)(2,1)} %bitcast.45, bf16[512,384]{1,0:T(8,128)(2,1)} %bitcast.46, bf16[512,1536]{1,0:T(8,128)(2,1)} %bitcast.42, bf16[512,1536]{1,0:T(8,128)(2,1)} %bitcast.43), custom_call_target="tpu_custom_call" | custom-call | flops 3623878656 | bytes 8388608 | tf_op jit(solution)/shard_map/weights/pallas_call | solution.py:131
  96.7 3.4 %copy.24 = bf16[2,16,24,1536]{3,2,0,1:T(8,128)(2,1)} copy(bf16[2,16,24,1536]{3,2,1,0:T(8,128)(2,1)} %bitcast.39) | data formatting | bytes 4718592 | tf_op jit(solution)/shard_map/reshape | solution.py:201
  100.0 0.1 all-to-all-done.1
  100.2 0.7 copy-done.7
  100.9 7.0 %all-to-all-start.3 = ((bf16[16,2,24,1536]{3,2,1,0:T(8,128)(2,1)}), bf16[16,2,24,1536]{3,2,1,0:T(8,128)(2,1)S(1)}, u32[]{:S(2)}, u32[]{:S(2)}) async-start(bf16[16,2,24,1536]{3,2,1,0:T(8,128)(2,1)} %bitcast.37), calls=%async_computation.3 | async-start | bytes 4718592 | tf_op jit(solution)/shard_map/all_to_all | solution.py:183
  107.9 1.6 convert_reduce_fusion.1
  109.5 1.5 all_to_all.24
  111.0 51.8 %all-to-all-done.3 = bf16[16,2,24,1536]{3,2,1,0:T(8,128)(2,1)S(1)} async-done(((bf16[16,2,24,1536]{3,2,1,0:T(8,128)(2,1)}), bf16[16,2,24,1536]{3,2,1,0:T(8,128)(2,1)S(1)}, u32[]{:S(2)}, u32[]{:S(2)}) %all-to-all-start.3) | async-done | bytes 2359328 | tf_op jit(solution)/shard_map/all_to_all | solution.py:183
  162.8 7.1 %all-to-all-start.2 = ((f32[16,1,576]{2,1,0:T(1,128)}), f32[16,1,576]{2,1,0:T(1,128)}, u32[]{:S(2)}, u32[]{:S(2)}) async-start(f32[16,1,576]{2,1,0:T(1,128)} %all_to_all.24), calls=%async_computation.2 | async-start | bytes 81920 | tf_op jit(solution)/shard_map/all_to_all | solution.py:183
  170.0 1.0 convert_reduce_fusion
  171.0 1.0 reshape.47
  172.0 0.9 copy.22
  173.0 3.3 %all-to-all-done.2 = f32[16,1,576]{2,1,0:T(1,128)} async-done(((f32[16,1,576]{2,1,0:T(1,128)}), f32[16,1,576]{2,1,0:T(1,128)}, u32[]{:S(2)}, u32[]{:S(2)}) %all-to-all-start.2) | async-done | bytes 36896 | tf_op jit(solution)/shard_map/all_to_all | solution.py:183
  176.3 4.8 %all-to-all-start.4 = ((f32[16,2,2304]{2,1,0:T(2,128)}), f32[16,2,2304]{2,1,0:T(2,128)S(1)}, u32[]{:S(2)}, u32[]{:S(2)}) async-start(f32[16,2,2304]{2,1,0:T(2,128)} %copy.22), calls=%async_computation.4 | async-start | bytes 589824 | tf_op jit(solution)/shard_map/all_to_all | solution.py:183
  181.1 3.5 %convolution_bitcast_fusion = f32[1,512,384]{2,1,0:T(8,128)} fusion(f32[384,384]{1,0:T(8,128)} %param.16, bf16[512,384]{1,0:T(8,128)(2,1)} %copy-done.6, bf16[512,384]{1,0:T(8,128)(2,1)} %copy-done.5, bf16[512,384]{1,0:T(8,128)(2,1)} %copy-done.4, f32[512,384]{1,0:T(8,128)} %get-tuple-element.12, bf16[512,384]{1,0:T(8,128)(2,1)S(1)} %collective-permute-done), kind=kOutput, calls=%fused_computation.2 | convolution fusion | flops 454557696 | bytes 3735552 | tf_op jit(solution)/shard_map/bg,fg->bf/dot_general | solution.py:214
  184.6 1.4 reduce_sum.37
  186.0 2.1 %all-to-all-done.4 = f32[16,2,2304]{2,1,0:T(2,128)S(1)} async-done(((f32[16,2,2304]{2,1,0:T(2,128)}), f32[16,2,2304]{2,1,0:T(2,128)S(1)}, u32[]{:S(2)}, u32[]{:S(2)}) %all-to-all-start.4) | async-done | bytes 294944 | tf_op jit(solution)/shard_map/all_to_all | solution.py:183
  188.1 0.1 reduce_sum.39
  188.2 0.6 slice_reduce_fusion
  (6 shorter events, 0.0 us)
Async XLA Ops:
  0.6 82.7 %copy-start = (f32[1,512,384]{2,1,0:T(8,128)S(1)}, f32[1,512,384]{2,1,0:T(8,128)}, u32[]{:S(2)}) copy-start(f32[1,512,384]{2,1,0:T(8,128)} %param.17) | copy-start | bytes 2359300
  0.6 3.2 %copy-start.2 = (f32[384,1536]{1,0:T(8,128)S(1)}, f32[384,1536]{1,0:T(8,128)}, u32[]{:S(2)}) copy-start(f32[384,1536]{1,0:T(8,128)} %param.14) | copy-start | bytes 7077892
  5.8 24.7 %copy-start.8 = (s32[1,1,5]{2,1,0:T(1,128)S(1)}, s32[1,1,5]{2,1,0:T(1,128)}, u32[]{:S(2)}) copy-start(s32[1,1,5]{2,1,0:T(1,128)} %param.19) | copy-start | bytes 64
  21.9 22.3 %all-to-all-start = ((bf16[16,32,384]{2,1,0:T(8,128)(2,1)}), bf16[16,32,384]{2,1,0:T(8,128)(2,1)S(1)}, u32[]{:S(2)}, u32[]{:S(2)}) async-start(bf16[16,32,384]{2,1,0:T(8,128)(2,1)} %get-tuple-element.11), calls=%async_computation | async-start | bytes 786432 | tf_op jit(solution)/shard_map/all_to_all | solution.py:197
  44.2 0.7 copy-start.3
  49.5 33.8 %copy-start.1 = (f32[512,384]{1,0:T(8,128)S(1)}, f32[512,384]{1,0:T(8,128)}, u32[]{:S(2)}) copy-start(f32[512,384]{1,0:T(8,128)} %get-tuple-element.12) | copy-start | bytes 2359300
  51.0 15.1 %collective-permute-start = (bf16[512,384]{1,0:T(8,128)(2,1)S(1)}, bf16[512,384]{1,0:T(8,128)(2,1)S(1)}, u32[]{:S(2)}, u32[]{:S(2)}) collective-permute-start(bf16[512,384]{1,0:T(8,128)(2,1)S(1)} %get-tuple-element.20), channel_id=1, source_target_pairs={{2,0},{3,1},{4,2},{5,3},{6,4},{7,5},{8,6},{9,7},{10,8},{11,9},{12,... | collective-permute-start | bytes 1179656 | tf_op jit(solution)/shard_map/ppermute | solution.py:179
  55.9 18.7 %collective-permute-start.1 = (bf16[512,384]{1,0:T(8,128)(2,1)S(1)}, bf16[512,384]{1,0:T(8,128)(2,1)S(1)}, u32[]{:S(2)}, u32[]{:S(2)}) collective-permute-start(bf16[512,384]{1,0:T(8,128)(2,1)S(1)} %get-tuple-element.23), channel_id=1, source_target_pairs={{1,0},{2,1},{3,2},{4,3},{5,4},{6,5},{7,6},{8,7},{9,8},{10,9},{11,1... | collective-permute-start | bytes 1179656 | tf_op jit(solution)/shard_map/ppermute | solution.py:179
  58.9 24.4 %collective-permute-start.2 = (bf16[512,384]{1,0:T(8,128)(2,1)S(1)}, bf16[512,384]{1,0:T(8,128)(2,1)S(1)}, u32[]{:S(2)}, u32[]{:S(2)}) collective-permute-start(bf16[512,384]{1,0:T(8,128)(2,1)S(1)} %get-tuple-element.22), channel_id=1, source_target_pairs={{0,1},{1,2},{2,3},{3,4},{4,5},{5,6},{6,7},{7,8},{8,9},{9,10},{10,1... | collective-permute-start | bytes 1179656 | tf_op jit(solution)/shard_map/ppermute | solution.py:179
  61.7 21.6 %collective-permute-start.3 = (bf16[512,384]{1,0:T(8,128)(2,1)S(1)}, bf16[512,384]{1,0:T(8,128)(2,1)S(1)}, u32[]{:S(2)}, u32[]{:S(2)}) collective-permute-start(bf16[512,384]{1,0:T(8,128)(2,1)S(1)} %get-tuple-element.21), channel_id=1, source_target_pairs={{0,2},{1,3},{2,4},{3,5},{4,6},{5,7},{6,8},{7,9},{8,10},{9,11},{10,... | collective-permute-start | bytes 1179656 | tf_op jit(solution)/shard_map/ppermute | solution.py:179
  74.6 10.4 %copy-start.4 = (bf16[512,384]{1,0:T(8,128)(2,1)}, bf16[512,384]{1,0:T(8,128)(2,1)S(1)}, u32[]{:S(2)}) copy-start(bf16[512,384]{1,0:T(8,128)(2,1)S(1)} %collective-permute-done.1) | copy-start | bytes 1179652
  83.3 1.7 copy-start.5
  83.3 1.7 copy-start.6
  85.0 15.2 %all-to-all-start.1 = ((bf16[16,24,384]{2,1,0:T(8,128)(2,1)}), bf16[16,24,384]{2,1,0:T(8,128)(2,1)S(1)}, u32[]{:S(2)}, u32[]{:S(2)}) async-start(bf16[16,24,384]{2,1,0:T(8,128)(2,1)} %bitcast.12), calls=%async_computation.1 | async-start | bytes 589824 | tf_op jit(solution)/shard_map/all_to_all | solution.py:183
  100.2 0.7 copy-start.7
  100.9 61.9 %all-to-all-start.3 = ((bf16[16,2,24,1536]{3,2,1,0:T(8,128)(2,1)}), bf16[16,2,24,1536]{3,2,1,0:T(8,128)(2,1)S(1)}, u32[]{:S(2)}, u32[]{:S(2)}) async-start(bf16[16,2,24,1536]{3,2,1,0:T(8,128)(2,1)} %bitcast.37), calls=%async_computation.3 | async-start | bytes 4718592 | tf_op jit(solution)/shard_map/all_to_all | solution.py:183
  162.8 13.5 %all-to-all-start.2 = ((f32[16,1,576]{2,1,0:T(1,128)}), f32[16,1,576]{2,1,0:T(1,128)}, u32[]{:S(2)}, u32[]{:S(2)}) async-start(f32[16,1,576]{2,1,0:T(1,128)} %all_to_all.24), calls=%async_computation.2 | async-start | bytes 81920 | tf_op jit(solution)/shard_map/all_to_all | solution.py:183
  176.3 11.8 %all-to-all-start.4 = ((f32[16,2,2304]{2,1,0:T(2,128)}), f32[16,2,2304]{2,1,0:T(2,128)S(1)}, u32[]{:S(2)}, u32[]{:S(2)}) async-start(f32[16,2,2304]{2,1,0:T(2,128)} %copy.22), calls=%async_computation.4 | async-start | bytes 589824 | tf_op jit(solution)/shard_map/all_to_all | solution.py:183

commit v2 on v1

v2 whole, which is shorter than its diff:
```python
import jax
import jax.numpy as jnp
from jax import lax
from jax.experimental import pallas as pl
from jax.experimental.pallas import tpu as pltpu
from jax.sharding import PartitionSpec as P

F32, BF16 = jnp.float32, jnp.bfloat16
VMEM_CAP = 62 * 1024 * 1024
COL_BLOCKS = 3
GROUP = 4
MESH = pl.DeviceIdType.MESH


def halves(value):
    high = value.astype(BF16)
    return high, (value - high.astype(F32)).astype(BF16)


def split_store(value, hi_ref, lo_ref):
    hi_ref[...], lo_ref[...] = halves(value)


def dot3(a_hi, a_lo, b_hi, b_lo, dims):
    one = lambda a, b: lax.dot_general(a, b, (dims, ((), ())), preferred_element_type=F32)
    return one(a_hi, b_hi) + (one(a_lo, b_hi) + one(a_hi, b_lo))


def remote(src, dst, send, recv, device):
    return pltpu.make_async_remote_copy(
        src_ref=src, dst_ref=dst, send_sem=send, recv_sem=recv, device_id=device, device_id_type=MESH
    )


def whole_kernel(
    present, gates, cells, grads, recur, input_any, conv_out_any, tiles_any, feats_any, conv_w_any,
    feat_out, conv_out_sum, lstm_sum,
    input_w, conv_out, tiles, feats, conv_w,
    r_hi, r_lo, i_hi, i_lo, rec, cell_grad,
    pre_hi, pre_lo, hid_hi, hid_lo, c_hi, c_lo, rounded, arrived,
    terms, pair_out, pair_in, z_out, z_in, full, x_out, x_in,
    away, got, z_grad, z_hi, z_lo, w_hi, w_lo, n_hi, n_lo,
    ct, cp_out, cp_in, cz_out, cz_in, cx_out, cx_in,
    load_sem, a_send, a_recv, p_send, p_recv, z_send, z_recv, x_send, x_recv,
    t_send, t_recv, cp_send, cp_recv, cz_send, cz_recv, cx_send, cx_recv,
):
    steps, rows, feat = cells.shape
    wide = 4 * feat
    snaps, verts = steps, x_out.shape[0]
    chips = snaps // 2
    own = feat // snaps
    slots = tiles.shape[0]
    reach = slots // 2
    width = wide // COL_BLOCKS
    me, mv = lax.axis_index("snap"), lax.axis_index("vert")
    chip, core = me // 2, me % 2
    mate = 2 * chip + 1 - core

    loads = [
        pltpu.make_async_copy(src, dst, load_sem.at[n])
        for n, (src, dst) in enumerate([
            (input_any, input_w), (conv_out_any, conv_out), (tiles_any, tiles),
            (feats_any, feats), (conv_w_any, conv_w),
        ])
    ]
    for load in loads:
        load.start()

    barrier = pltpu.get_barrier_semaphore()
    for s in range(snaps):
        @pl.when(s != me)
        def _():
            pl.semaphore_signal(barrier, inc=1, device_id=(s, mv), device_id_type=MESH)
    for v in range(verts):
        @pl.when(v != mv)
        def _():
            pl.semaphore_signal(barrier, inc=1, device_id=(me, v), device_id_type=MESH)

    for k in range(4):
        cols = slice(k * feat, (k + 1) * feat)
        split_store(recur[:, cols].T, r_hi.at[cols, :], r_lo.at[cols, :])
    loads[0].wait()
    for k in range(4):
        cols = slice(k * feat, (k + 1) * feat)
        split_store(input_w[:, cols].T, i_hi.at[cols, :], i_lo.at[cols, :])
    rec[...] = jnp.zeros_like(rec)
    cell_grad[...] = jnp.zeros_like(cell_grad)
    pl.semaphore_wait(barrier, snaps + verts - 2)

    def step(t):
        before = jnp.maximum(t - 1, 0)
        live = (t > 0).astype(F32)
        part = lambda k: gates[t, :, k * feat : (k + 1) * feat].astype(F32)
        in_gate, forget, candidate, out_gate = part(0), part(1), part(2), part(3)
        squashed = jnp.tanh(cells[t].astype(F32))
        cell_before = cells[before].astype(F32) * live
        hidden = gates[before, :, 3 * feat :].astype(F32) * jnp.tanh(cell_before)
        hid_hi[t], hid_lo[t] = halves(hidden)
        total = grads[t] + rec[...]
        cell_total = cell_grad[...] + total * (out_gate * (1.0 - squashed * squashed))
        pieces = [
            cell_total * (candidate * in_gate * (1.0 - in_gate)),
            cell_total * (cell_before * forget * (1.0 - forget)),
            cell_total * (in_gate * (1.0 - candidate * candidate)),
            total * (squashed * out_gate * (1.0 - out_gate)),
        ]
        cell_grad[...] = cell_total * forget
        acc = None
        for k, piece in enumerate(pieces):
            cols = slice(k * feat, (k + 1) * feat)
            high, low = halves(piece)
            pre_hi[t, :, cols] = high
            pre_lo[t, :, cols] = low
            both = jnp.concatenate([high, low], axis=0)
            main = jnp.dot(both, r_hi[cols, :], preferred_element_type=F32)
            side = jnp.dot(high, r_lo[cols, :], preferred_element_type=F32)
            term = main[:rows] + (main[rows:] + side)
            acc = term if acc is None else acc + term
        rec[...] = acc

    def give(t):
        return remote(rounded.at[t], arrived.at[me], a_send.at[t], a_recv.at[me], (t, mv))

    def group(n, carry):
        base = steps - GROUP * (n + 1)

        def inner(j, c):
            step(base + GROUP - 1 - j)
            return c

        lax.fori_loop(0, GROUP, inner, 0)
        shape = (GROUP * rows, wide)
        value = dot3(
            pre_hi[pl.ds(base, GROUP)].reshape(shape), pre_lo[pl.ds(base, GROUP)].reshape(shape),
            i_hi[...], i_lo[...], ((1,), (0,)),
        )
        rounded[pl.ds(base, GROUP)] = value.astype(BF16).reshape(GROUP, rows, feat)
        for j in range(GROUP):
            t = base + j

            @pl.when(t != me)
            def _():
                give(t).start()
        return carry

    lax.fori_loop(0, steps // GROUP, group, 0)
    arrived[me] = rounded[me]

    loads[1].wait()
    flat = lambda ref: ref[...].reshape(steps * rows, feat)
    split_store(flat(conv_out), c_hi, c_lo)
    first = ((0,), (0,))

    def pair_copy(n):
        return remote(pair_out.at[n], pair_in.at[n], p_send.at[n], p_recv.at[n], (mate, mv))

    def along_z(n, q):
        return remote(
            z_out.at[n, q], z_in.at[n, chip], z_send.at[n, q], z_recv.at[n, chip], (2 * q + core, mv)
        )

    def from_z(n, q):
        return remote(
            z_out.at[n, q], z_in.at[n, q], z_send.at[n, q], z_recv.at[n, q], (2 * q + core, mv)
        )

    def make_terms(n):
        cols = slice(n * width, (n + 1) * width)
        p_hi = pre_hi[:, :, cols].reshape(steps * rows, width)
        p_lo = pre_lo[:, :, cols].reshape(steps * rows, width)
        value = dot3(c_hi[...], c_lo[...], p_hi, p_lo, first)
        terms[n, :, 0:own, :] = value.reshape(snaps, own, width)
        value = dot3(flat(hid_hi), flat(hid_lo), p_hi, p_lo, first)
        terms[n, :, own : 2 * own, :] = value.reshape(snaps, own, width)
        for q in range(chips):
            pair_out[n, q] = terms[n, 2 * q + 1 - core].astype(BF16)
        pair_copy(n).start()

    def chip_sum(n, q):
        return terms[n, 2 * q + core] + pair_in[n, q].astype(F32)

    def send_z(n):
        pair_copy(n).wait_recv()
        for q in range(chips):
            z_out[n, q] = chip_sum(n, q).astype(BF16)
        for q in range(chips):
            @pl.when(q != chip)
            def _():
                along_z(n, q).start()

    for n in range(COL_BLOCKS):
        make_terms(n)
        if n > 0:
            send_z(n - 1)

    for s in range(snaps):
        @pl.when(s != me)
        def _():
            remote(rounded.at[s], arrived.at[s], a_send.at[s], a_recv.at[s], (s, mv)).wait_recv()
    loads[2].wait()
    block = steps * rows
    mine = arrived[...].reshape(block, feat)

    def partial_copy(slot):
        return remote(
            away.at[slot], got.at[slot], t_send.at[slot], t_recv.at[slot], (me, mv + slot - reach)
        )

    def has_target(slot):
        return (mv + (slot - reach) >= 0) & (mv + (slot - reach) < verts)

    def has_source(slot):
        return (mv - (slot - reach) >= 0) & (mv - (slot - reach) < verts)

    ordered = [s for d in range(reach, 0, -1) for s in (reach - d, reach + d)]
    for slot in ordered + [reach]:
        value = lax.dot_general(
            tiles[slot], mine, (first, ((), ())), preferred_element_type=F32
        ) * present[slot].astype(F32)
        if slot == reach:
            z_grad[...] = value
        else:
            away[slot] = value.astype(BF16)

            @pl.when(has_target(slot))
            def _():
                partial_copy(slot).start()
            if slot == ordered[0]:
                send_z(COL_BLOCKS - 1)

    loads[3].wait()
    loads[4].wait()
    split_store(feats[...], n_hi, n_lo)
    split_store(conv_w[...], w_hi, w_lo)
    for slot in ordered[::-1]:
        @pl.when(has_source(slot))
        def _():
            partial_copy(slot).wait_recv()
            z_grad[...] += got[slot].astype(F32)
    split_store(z_grad[...], z_hi, z_lo)

    ct[...] = dot3(n_hi[...], n_lo[...], z_hi[...], z_lo[...], first).reshape(snaps, own, feat)
    for q in range(chips):
        cp_out[q] = ct[2 * q + 1 - core]
    conv_pair = remote(cp_out, cp_in, cp_send, cp_recv, (mate, mv))
    conv_pair.start()

    def conv_z(q, landing):
        return remote(
            cz_out.at[q], cz_in.at[landing], cz_send.at[q], cz_recv.at[landing], (2 * q + core, mv)
        )

    feat_out[...] = dot3(z_hi[...], z_lo[...], w_hi[...], w_lo[...], ((1,), (1,)))
    conv_pair.wait_recv()
    for q in range(chips):
        cz_out[q] = ct[2 * q + core] + cp_in[q]
    for q in range(chips):
        @pl.when(q != chip)
        def _():
            conv_z(q, chip).start()

    x_out[...] = jnp.zeros_like(x_out)
    for n in range(COL_BLOCKS):
        cols = slice(n * width, (n + 1) * width)
        full[:, cols] = chip_sum(n, chip)
        for q in range(chips):
            @pl.when(q != chip)
            def _():
                from_z(n, q).wait_recv()
                full[:, cols] += z_in[n, q].astype(F32)
    half = wide // 2
    share = 2 * own // verts
    for v in range(verts):
        for g in range(2):
            for j in range(share):
                h = share * v + j
                row = g * own + h // 2
                col = (h % 2) * half
                x_out[v, g * share + j : g * share + j + 1, :] = full[row : row + 1, col : col + half]

    def along_v(v, landing):
        return remote(x_out.at[v], x_in.at[landing], x_send.at[v], x_recv.at[landing], (me, v))

    for v in range(verts):
        @pl.when(v != mv)
        def _():
            along_v(v, mv).start()

    cx_out[...] = jnp.zeros_like(cx_out)
    cz_in[chip] = cz_out[chip]
    for q in range(chips):
        @pl.when(q != chip)
        def _():
            conv_z(q, q).wait_recv()
    summed = cz_in[0]
    for q in range(1, chips):
        summed += cz_in[q]
    pairs = verts // 2
    for j in range(pairs):
        cx_out[j, 0:share, :] = summed[share * j : share * (j + 1), :]

    def conv_v(v, landing):
        return remote(cx_out.at[v // 2], cx_in.at[landing], cx_send.at[v], cx_recv.at[landing], (me, v))

    for v in range(verts):
        @pl.when(v != mv)
        def _():
            conv_v(v, mv).start()
    x_in[mv] = x_out[mv]
    cx_in[mv] = cx_out[mv // 2]
    for v in range(verts):
        @pl.when(v != mv)
        def _():
            along_v(v, v).wait_recv()
    lstm_sum[...] = jnp.sum(x_in[...], axis=0)
    for v in range(verts):
        @pl.when(v != mv)
        def _():
            conv_v(v, v).wait_recv()
    conv_out_sum[...] = jnp.sum(cx_in[...], axis=0)

    for s in range(snaps):
        @pl.when(s != me)
        def _():
            give(s).wait_send()
    for n in range(COL_BLOCKS):
        pair_copy(n).wait_send()
        for q in range(chips):
            @pl.when(q != chip)
            def _():
                along_z(n, q).wait_send()
    for slot in ordered:
        @pl.when(has_target(slot))
        def _():
            partial_copy(slot).wait_send()
    conv_pair.wait_send()
    for q in range(chips):
        @pl.when(q != chip)
        def _():
            conv_z(q, chip).wait_send()
    for v in range(verts):
        @pl.when(v != mv)
        def _():
            along_v(v, mv).wait_send()
            conv_v(v, mv).wait_send()


def run_whole(
    present, gates, cells, grads, recur, input_w, conv_out, tiles, feats, conv_w, snaps, verts
):
    steps, rows, feat = cells.shape
    wide = 4 * feat
    slots, block, _ = tiles.shape
    chips, own, width = snaps // 2, feat // snaps, wide // COL_BLOCKS
    share = 2 * own // verts
    total = steps * rows
    vm = pl.BlockSpec(memory_space=pltpu.VMEM)
    hbm = pl.BlockSpec(memory_space=pl.ANY)
    b = lambda *s: pltpu.VMEM(s, BF16)
    f = lambda *s: pltpu.VMEM(s, F32)
    sem = lambda *s: pltpu.SemaphoreType.DMA(s)
    like = lambda a: pltpu.VMEM(a.shape, a.dtype)
    conv_rows = -(-share // 8) * 8
    lstm_rows = -(-2 * share // 8) * 8
    return pl.pallas_call(
        whole_kernel,
        in_specs=[pl.BlockSpec(memory_space=pltpu.SMEM)] + [vm] * 4 + [hbm] * 5,
        out_specs=[vm] * 3,
        out_shape=[
            jax.ShapeDtypeStruct((block, feat), F32),
            jax.ShapeDtypeStruct((conv_rows, feat), F32),
            jax.ShapeDtypeStruct((lstm_rows, wide // 2), F32),
        ],
        scratch_shapes=[
            like(input_w), like(conv_out), like(tiles), like(feats), like(conv_w),
            b(wide, feat), b(wide, feat), b(wide, feat), b(wide, feat), f(rows, feat), f(rows, feat),
            b(steps, rows, wide), b(steps, rows, wide), b(steps, rows, feat), b(steps, rows, feat),
            b(total, feat), b(total, feat), b(steps, rows, feat), b(steps, rows, feat),
            f(COL_BLOCKS, snaps, 2 * own, width),
            b(COL_BLOCKS, chips, 2 * own, width), b(COL_BLOCKS, chips, 2 * own, width),
            b(COL_BLOCKS, chips, 2 * own, width), b(COL_BLOCKS, chips, 2 * own, width),
            f(2 * own, wide), f(verts, lstm_rows, wide // 2), f(verts, lstm_rows, wide // 2),
            b(slots, block, feat), b(slots, block, feat), f(block, feat), b(block, feat), b(block, feat),
            b(feat, feat), b(feat, feat), b(block, feat), b(block, feat),
            f(snaps, own, feat), f(chips, own, feat), f(chips, own, feat),
            f(chips, own, feat), f(chips, own, feat),
            f(verts // 2, conv_rows, feat), f(verts, conv_rows, feat),
            sem(5), sem(snaps), sem(snaps), sem(COL_BLOCKS), sem(COL_BLOCKS),
            sem(COL_BLOCKS, chips), sem(COL_BLOCKS, chips), sem(verts), sem(verts),
            sem(slots), sem(slots), pltpu.SemaphoreType.DMA, pltpu.SemaphoreType.DMA,
            sem(chips), sem(chips), sem(verts), sem(verts),
        ],
        compiler_params=pltpu.CompilerParams(
            vmem_limit_bytes=VMEM_CAP, collective_id=0, has_side_effects=True
        ),
        name="whole",
    )(present, gates, cells, grads, recur, input_w, conv_out, tiles, feats, conv_w)


def local(
    saved_gates, saved_cells, conv_out, out_grad, input_weight, recur_weight,
    conv_weight, node_feats, tile_values, tile_mask,
):
    feat = saved_cells.shape[-1]
    snaps, verts = lax.axis_size("snap"), lax.axis_size("vert")
    slot_count = tile_values.shape[2]
    reach = slot_count // 2
    mv = lax.axis_index("vert")
    target = mv + jnp.arange(slot_count, dtype=jnp.int32) - reach
    inside = (target >= 0) & (target < verts)
    present = ((tile_mask[0, 0] == 1) & inside).astype(jnp.int32)
    feat_grad, conv, lstm = run_whole(
        present, saved_gates, saved_cells, out_grad, recur_weight, input_weight, conv_out,
        tile_values[0, 0], node_feats[0], conv_weight, snaps, verts,
    )
    share = 2 * (feat // snaps) // verts
    size = share * feat // 2
    conv = lax.dynamic_slice_in_dim(conv[:share].reshape(-1), (mv % 2) * size, size)
    return (
        feat_grad[None],
        conv,
        lstm[:share].reshape(-1),
        lstm[share : 2 * share].reshape(-1),
    )


def solution(mesh):
    along = P(None, ("vert", "snap"), None)
    placed = (
        along, along, along, along, P(), P(), P(),
        P("snap", "vert", None), P("snap", "vert", None, None, None), P("snap", "vert", None),
    )
    both = P(("snap", "vert"))
    return jax.shard_map(
        local,
        mesh=mesh,
        in_specs=placed,
        out_specs=(P("snap", "vert", None), both, both, both),
        check_vma=False,
    )
```

time: 190 us -> 88 us (0.46)
  waiting for transfers between devices: 89.5 us -> 0 us
  Pallas kernels: 28.7 us -> 79.1 us
  starting transfers between devices: 44.3 us -> 0 us
  local copies, waits for them, and re-layouts: 15.7 us -> 5.48 us
  matrix products: 5.16 us -> 0 us
  other arithmetic: 4.68 us -> 1.17 us
    all_to_all x5 -> x0, waiting for transfers between devices: 70.6 us -> none  [the longest x4 57.4 us: summed_pieces(): got = lax.all_to_all(pieces, axis, split_axis=0, concat_axis=0, tiled=True)]
    pallas_call x3 -> x1, Pallas kernels: 28.7 us -> 79.1 us  [run_whole(): pl.pallas_call(whole_kernel, in_specs=[pl.BlockSpec(memory_space=pltpu.SM...]
    all_to_all x5 -> x0, starting transfers between devices: 31 us -> none  [the longest x4 22.5 us: summed_pieces(): got = lax.all_to_all(pieces, axis, split_axis=0, concat_axis=0, tiled=True)]
    ppermute x4 -> x0, waiting for transfers between devices: 18.9 us -> none  [passed_along(): return lax.ppermute(shard, axis, pairs)]
    ppermute x4 -> x0, starting transfers between devices: 13.3 us -> none  [passed_along(): return lax.ppermute(shard, axis, pairs)]
    dot_general x2 -> x0, matrix products: 5.16 us -> none  [the longest x1 3.49 us: local(): jnp.einsum('bg,fg->bf', z_grad, conv_weight, precision=lax.Precision.HIGH...]
    unnamed x20 -> x1, local copies, waits for them, and re-layouts: 6.68 us -> 2.06 us
    reduce_sum x4 -> x0, other arithmetic: 4.16 us -> none  [summed_pieces(): return jnp.sum(got.astype(F32), axis=0)]
  transfers between devices with their start and end apart: 9 -> 0, of which waited for: 8 -> 0; matrix products, arithmetic and copies ran while one was open for 7% -> 0% of each run, Pallas kernels for 4% -> 0%
where the time goes in v2:
time: 88 us; the launch traced here: 86.5 us
  Pallas kernels  79.1 us (90%)
  local copies, waits for them, and re-layouts  5.48 us (6%)
  other arithmetic  1.17 us (1%)
    pallas_call x1, Pallas kernels, run_whole(): pl.pallas_call(whole_kernel, in_specs=[pl.BlockSpec(memory_space=pltpu.SM...  79.1 us
    unnamed x1, local copies, waits for them, and re-layouts  2.06 us

profile of v2, /device:TPU:8, one launch (start us, length us, event | category | flops | bytes accessed | tf_op | source)
XLA Modules:
  0.0 86.5 jit_solution(9675828351796918239)
XLA Ops:
  0.6 1.2 %fusion.present = s32[5]{0:T(128)} fusion(s32[1,1,5]{2,1,0:T(1,128)} %param.19, s32[]{:T(128)S(6)} %axis_index.12), kind=kLoop, calls=%fused_computation.1 | loop fusion | flops 40 | bytes 44 | tf_op jit(solution)/shard_map/convert_element_type | solution.py:411
  1.8 79.1 %whole.1 = (f32[512,384]{1,0:T(8,128)}, f32[8,384]{1,0:T(8,128)}, f32[8,768]{1,0:T(8,128)}) custom-call(s32[5]{0:T(128)} %fusion.present, bf16[16,32,1536]{2,1,0:T(8,128)(2,1)} %gates.1, bf16[16,32,384]{2,1,0:T(8,128)(2,1)} %cells.1, f32[16,32,384]{2,1,0:T(8,128)} %grads.1, f32[384,1536]{1,0:T(8,128)} %recur.1, f32[384,1536]{1,0:T(8,128)} %input_any.1, ...), custom_call_target="tpu_custom_call" | custom-call | tf_op jit(solution)/shard_map/whole/pallas_call | solution.py:365
  81.0 0.7 slice.9
  81.7 0.7 dynamic_slice.3
  82.4 0.8 fusion.1
  83.2 0.6 reshape.20
  83.8 0.6 reshape.21
  84.4 2.1 %copy.15 = f32[1,512,384]{2,1,0:T(8,128)} copy(f32[1,512,384]{2,1,0:T(8,128)} %bitcast.9) | data formatting | bytes 1572864
  (1 shorter events, 0.0 us)

commit v3 on v2

--- a/solution.py
+++ b/solution.py
@@ -33,16 +33,16 @@
 
 
 def whole_kernel(
-    present, gates, cells, grads, recur, input_any, conv_out_any, tiles_any, feats_any, conv_w_any,
-    feat_out, conv_out_sum, lstm_sum,
+    mask, gates, cells, grads, recur, input_any, conv_out_any, tiles_any, feats_any, conv_w_any,
+    feat_out, sums_out,
     input_w, conv_out, tiles, feats, conv_w,
     r_hi, r_lo, i_hi, i_lo, rec, cell_grad,
     pre_hi, pre_lo, hid_hi, hid_lo, c_hi, c_lo, rounded, arrived,
     terms, pair_out, pair_in, z_out, z_in, full, x_out, x_in,
-    away, got, z_grad, z_hi, z_lo, w_hi, w_lo, n_hi, n_lo,
+    via_out, via_in, next_to, away, got, z_grad, z_hi, z_lo, w_hi, w_lo, n_hi, n_lo,
     ct, cp_out, cp_in, cz_out, cz_in, cx_out, cx_in,
     load_sem, a_send, a_recv, p_send, p_recv, z_send, z_recv, x_send, x_recv,
-    t_send, t_recv, cp_send, cp_recv, cz_send, cz_recv, cx_send, cx_recv,
+    v_send, v_recv, t_send, t_recv, cp_send, cp_recv, cz_send, cz_recv, cx_send, cx_recv,
 ):
     steps, rows, feat = cells.shape
     wide = 4 * feat
@@ -121,29 +121,32 @@
     def give(t):
         return remote(rounded.at[t], arrived.at[me], a_send.at[t], a_recv.at[me], (t, mv))
 
-    def group(n, carry):
-        base = steps - GROUP * (n + 1)
-
+    def group(base, size):
         def inner(j, c):
-            step(base + GROUP - 1 - j)
+            step(base + size - 1 - j)
             return c
 
-        lax.fori_loop(0, GROUP, inner, 0)
-        shape = (GROUP * rows, wide)
+        lax.fori_loop(0, size, inner, 0)
+        shape = (size * rows, wide)
         value = dot3(
-            pre_hi[pl.ds(base, GROUP)].reshape(shape), pre_lo[pl.ds(base, GROUP)].reshape(shape),
+            pre_hi[pl.ds(base, size)].reshape(shape), pre_lo[pl.ds(base, size)].reshape(shape),
             i_hi[...], i_lo[...], ((1,), (0,)),
         )
-        rounded[pl.ds(base, GROUP)] = value.astype(BF16).reshape(GROUP, rows, feat)
-        for j in range(GROUP):
+        rounded[pl.ds(base, size)] = value.astype(BF16).reshape(size, rows, feat)
+        for j in range(size):
             t = base + j
 
             @pl.when(t != me)
             def _():
                 give(t).start()
+
+    def full_group(n, carry):
+        group(steps - GROUP * (n + 1), GROUP)
         return carry
 
-    lax.fori_loop(0, steps // GROUP, group, 0)
+    lax.fori_loop(0, steps // GROUP - 1, full_group, 0)
+    group(GROUP // 2, GROUP // 2)
+    group(0, GROUP // 2)
     arrived[me] = rounded[me]
 
     loads[1].wait()
@@ -188,10 +191,7 @@
             def _():
                 along_z(n, q).start()
 
-    for n in range(COL_BLOCKS):
-        make_terms(n)
-        if n > 0:
-            send_z(n - 1)
+    make_terms(0)
 
     for s in range(snaps):
         @pl.when(s != me)
@@ -201,42 +201,78 @@
     block = steps * rows
     mine = arrived[...].reshape(block, feat)
 
-    def partial_copy(slot):
+    parts_of = 2
+    chunk = block // parts_of
+
+    def near(d):
+        return (mv + d >= 0) & (mv + d < verts)
+
+    def via_copy(d, k):
+        at = pl.ds(k * chunk, chunk)
+        w = (d + 1) // 2
         return remote(
-            away.at[slot], got.at[slot], t_send.at[slot], t_recv.at[slot], (me, mv + slot - reach)
+            via_out.at[w, at], via_in.at[w, at], v_send.at[w, k], v_recv.at[w, k], (me, mv + d)
         )
 
-    def has_target(slot):
-        return (mv + (slot - reach) >= 0) & (mv + (slot - reach) < verts)
-
-    def has_source(slot):
-        return (mv - (slot - reach) >= 0) & (mv - (slot - reach) < verts)
-
-    ordered = [s for d in range(reach, 0, -1) for s in (reach - d, reach + d)]
-    for slot in ordered + [reach]:
-        value = lax.dot_general(
+    def sum_copy(d, k):
+        at = pl.ds(k * chunk, chunk)
+        w = (d + 1) // 2
+        return remote(away.at[w, at], got.at[w, at], t_send.at[w, k], t_recv.at[w, k], (me, mv + d))
+
+    def product(slot):
+        return lax.dot_general(
             tiles[slot], mine, (first, ((), ())), preferred_element_type=F32
-        ) * present[slot].astype(F32)
-        if slot == reach:
-            z_grad[...] = value
-        else:
-            away[slot] = value.astype(BF16)
-
-            @pl.when(has_target(slot))
-            def _():
-                partial_copy(slot).start()
-            if slot == ordered[0]:
-                send_z(COL_BLOCKS - 1)
+        ) * (mask[0, 0, slot] == 1).astype(F32)
+
+    for d in (1, -1):
+        via_out[(d + 1) // 2] = product(reach + 2 * d).astype(BF16)
+
+        @pl.when(near(2 * d))
+        def _():
+            for k in range(parts_of):
+                via_copy(d, k).start()
+    send_z(0)
+    for d in (1, -1):
+        next_to[(d + 1) // 2] = product(reach + d)
+
+    def pass_on(k):
+        at = pl.ds(k * chunk, chunk)
+        for d in (1, -1):
+            w = (d + 1) // 2
+
+            @pl.when(near(d) & near(-d))
+            def _():
+                via_copy(d, k).wait_recv()
+                away[w, at] = (next_to[w, at] + via_in[w, at].astype(F32)).astype(BF16)
+
+            @pl.when(near(d) & jnp.logical_not(near(-d)))
+            def _():
+                away[w, at] = next_to[w, at].astype(BF16)
+
+            @pl.when(near(d))
+            def _():
+                sum_copy(d, k).start()
+
+    make_terms(1)
+    pass_on(0)
+    for n in range(2, COL_BLOCKS):
+        send_z(n - 1)
+        make_terms(n)
+    pass_on(1)
+    send_z(COL_BLOCKS - 1)
+    z_grad[...] = product(reach)
 
     loads[3].wait()
     loads[4].wait()
     split_store(feats[...], n_hi, n_lo)
     split_store(conv_w[...], w_hi, w_lo)
-    for slot in ordered[::-1]:
-        @pl.when(has_source(slot))
-        def _():
-            partial_copy(slot).wait_recv()
-            z_grad[...] += got[slot].astype(F32)
+    for k in range(parts_of):
+        at = pl.ds(k * chunk, chunk)
+        for d in (1, -1):
+            @pl.when(near(-d))
+            def _():
+                sum_copy(d, k).wait_recv()
+                z_grad[at] += got[(d + 1) // 2, at].astype(F32)
     split_store(z_grad[...], z_hi, z_lo)
 
     ct[...] = dot3(n_hi[...], n_lo[...], z_hi[...], z_lo[...], first).reshape(snaps, own, feat)
@@ -253,7 +289,7 @@
     feat_out[...] = dot3(z_hi[...], z_lo[...], w_hi[...], w_lo[...], ((1,), (1,)))
     conv_pair.wait_recv()
     for q in range(chips):
-        cz_out[q] = ct[2 * q + core] + cp_in[q]
+        cz_out[q] = (ct[2 * q + core] + cp_in[q]).astype(BF16)
     for q in range(chips):
         @pl.when(q != chip)
         def _():
@@ -292,9 +328,9 @@
         @pl.when(q != chip)
         def _():
             conv_z(q, q).wait_recv()
-    summed = cz_in[0]
+    summed = cz_in[0].astype(F32)
     for q in range(1, chips):
-        summed += cz_in[q]
+        summed += cz_in[q].astype(F32)
     pairs = verts // 2
     for j in range(pairs):
         cx_out[j, 0:share, :] = summed[share * j : share * (j + 1), :]
@@ -312,12 +348,29 @@
         @pl.when(v != mv)
         def _():
             along_v(v, v).wait_recv()
-    lstm_sum[...] = jnp.sum(x_in[...], axis=0)
+    summed = jnp.sum(x_in[...], axis=0)
+    parts = half // 128
+    for n in range(2 * share):
+        for k in range(parts):
+            at = n * parts + k
+            sums_out[at : at + 1, :] = summed[n : n + 1, k * 128 : (k + 1) * 128]
     for v in range(verts):
         @pl.when(v != mv)
         def _():
             conv_v(v, v).wait_recv()
-    conv_out_sum[...] = jnp.sum(cx_in[...], axis=0)
+    summed = jnp.sum(cx_in[...], axis=0)
+    flat_rows = [
+        summed[n : n + 1, k * 128 : (k + 1) * 128] for n in range(share) for k in range(feat // 128)
+    ]
+    base, skip = 2 * share * parts, share * feat // 256
+    shift = share * feat // 2 - skip * 128
+    for n in range(skip + (1 if shift else 0)):
+        late = flat_rows[skip + n]
+        if shift and skip + n + 1 < len(flat_rows):
+            late = jnp.concatenate([late[:, shift:], flat_rows[skip + n + 1][:, :shift]], axis=1)
+        elif shift:
+            late = jnp.concatenate([late[:, shift:], late[:, :shift]], axis=1)
+        sums_out[base + n : base + n + 1, :] = jnp.where(mv % 2 == 0, flat_rows[n], late)
 
     for s in range(snaps):
         @pl.when(s != me)
@@ -329,10 +382,15 @@
             @pl.when(q != chip)
             def _():
                 along_z(n, q).wait_send()
-    for slot in ordered:
-        @pl.when(has_target(slot))
-        def _():
-            partial_copy(slot).wait_send()
+    for k in range(parts_of):
+        for d in (1, -1):
+            @pl.when(near(2 * d))
+            def _():
+                via_copy(d, k).wait_send()
+
+            @pl.when(near(d))
+            def _():
+                sum_copy(d, k).wait_send()
     conv_pair.wait_send()
     for q in range(chips):
         @pl.when(q != chip)
@@ -346,7 +404,7 @@
 
 
 def run_whole(
-    present, gates, cells, grads, recur, input_w, conv_out, tiles, feats, conv_w, snaps, verts
+    mask, gates, cells, grads, recur, input_w, conv_out, tiles, feats, conv_w, snaps, verts
 ):
     steps, rows, feat = cells.shape
     wide = 4 * feat
@@ -362,14 +420,14 @@
     like = lambda a: pltpu.VMEM(a.shape, a.dtype)
     conv_rows = -(-share // 8) * 8
     lstm_rows = -(-2 * share // 8) * 8
+    sum_rows = -(-(2 * share * wide // 256 + share * feat // 256 + 1) // 8) * 8
     return pl.pallas_call(
         whole_kernel,
         in_specs=[pl.BlockSpec(memory_space=pltpu.SMEM)] + [vm] * 4 + [hbm] * 5,
-        out_specs=[vm] * 3,
+        out_specs=[vm] * 2,
         out_shape=[
             jax.ShapeDtypeStruct((block, feat), F32),
-            jax.ShapeDtypeStruct((conv_rows, feat), F32),
-            jax.ShapeDtypeStruct((lstm_rows, wide // 2), F32),
+            jax.ShapeDtypeStruct((sum_rows, 128), F32),
         ],
         scratch_shapes=[
             like(input_w), like(conv_out), like(tiles), like(feats), like(conv_w),
@@ -380,21 +438,22 @@
             b(COL_BLOCKS, chips, 2 * own, width), b(COL_BLOCKS, chips, 2 * own, width),
             b(COL_BLOCKS, chips, 2 * own, width), b(COL_BLOCKS, chips, 2 * own, width),
             f(2 * own, wide), f(verts, lstm_rows, wide // 2), f(verts, lstm_rows, wide // 2),
-            b(slots, block, feat), b(slots, block, feat), f(block, feat), b(block, feat), b(block, feat),
+            b(2, block, feat), b(2, block, feat), f(2, block, feat), b(2, block, feat),
+            b(2, block, feat), f(block, feat), b(block, feat), b(block, feat),
             b(feat, feat), b(feat, feat), b(block, feat), b(block, feat),
             f(snaps, own, feat), f(chips, own, feat), f(chips, own, feat),
-            f(chips, own, feat), f(chips, own, feat),
+            b(chips, own, feat), b(chips, own, feat),
             f(verts // 2, conv_rows, feat), f(verts, conv_rows, feat),
             sem(5), sem(snaps), sem(snaps), sem(COL_BLOCKS), sem(COL_BLOCKS),
             sem(COL_BLOCKS, chips), sem(COL_BLOCKS, chips), sem(verts), sem(verts),
-            sem(slots), sem(slots), pltpu.SemaphoreType.DMA, pltpu.SemaphoreType.DMA,
+            sem(2, 2), sem(2, 2), sem(2, 2), sem(2, 2), pltpu.SemaphoreType.DMA, pltpu.SemaphoreType.DMA,
             sem(chips), sem(chips), sem(verts), sem(verts),
         ],
         compiler_params=pltpu.CompilerParams(
             vmem_limit_bytes=VMEM_CAP, collective_id=0, has_side_effects=True
         ),
         name="whole",
-    )(present, gates, cells, grads, recur, input_w, conv_out, tiles, feats, conv_w)
+    )(mask, gates, cells, grads, recur, input_w, conv_out, tiles, feats, conv_w)
 
 
 def local(
@@ -403,25 +462,15 @@
 ):
     feat = saved_cells.shape[-1]
     snaps, verts = lax.axis_size("snap"), lax.axis_size("vert")
-    slot_count = tile_values.shape[2]
-    reach = slot_count // 2
-    mv = lax.axis_index("vert")
-    target = mv + jnp.arange(slot_count, dtype=jnp.int32) - reach
-    inside = (target >= 0) & (target < verts)
-    present = ((tile_mask[0, 0] == 1) & inside).astype(jnp.int32)
-    feat_grad, conv, lstm = run_whole(
-        present, saved_gates, saved_cells, out_grad, recur_weight, input_weight, conv_out,
+    feat_grad, sums = run_whole(
+        tile_mask, saved_gates, saved_cells, out_grad, recur_weight, input_weight, conv_out,
         tile_values[0, 0], node_feats[0], conv_weight, snaps, verts,
     )
     share = 2 * (feat // snaps) // verts
     size = share * feat // 2
-    conv = lax.dynamic_slice_in_dim(conv[:share].reshape(-1), (mv % 2) * size, size)
-    return (
-        feat_grad[None],
-        conv,
-        lstm[:share].reshape(-1),
-        lstm[share : 2 * share].reshape(-1),
-    )
+    flat = sums.reshape(-1)
+    each = 4 * size
+    return (feat_grad[None], flat[2 * each : 2 * each + size], flat[:each], flat[each : 2 * each])
 
 
 def solution(mesh):

time: 88 us -> 80.3 us (0.912)
  the two profiles are of different devices: /device:TPU:8 before, /device:TPU:248 now
where the time goes in v3:
time: 80.3 us; the launch traced here: 79.9 us
  Pallas kernels  74.6 us (93%)
  local copies, waits for them, and re-layouts  4.74 us (6%)
    pallas_call x1, Pallas kernels, run_whole(): pl.pallas_call(whole_kernel, in_specs=[pl.BlockSpec(memory_space=pltpu.SM...  74.6 us
    unnamed x1, local copies, waits for them, and re-layouts  2.06 us

profile of v3, /device:TPU:248, one launch (start us, length us, event | category | flops | bytes accessed | tf_op | source)
XLA Modules:
  0.0 79.9 jit_solution(8816007494918365290)
XLA Ops:
  0.6 74.6 %whole.1 = (f32[512,384]{1,0:T(8,128)}, f32[48,128]{1,0:T(8,128)}) custom-call(s32[1,1,5]{2,1,0:T(1,128)} %mask.1, bf16[16,32,1536]{2,1,0:T(8,128)(2,1)} %gates.1, bf16[16,32,384]{2,1,0:T(8,128)(2,1)} %cells.1, f32[16,32,384]{2,1,0:T(8,128)} %grads.1, f32[384,1536]{1,0:T(8,128)} %recur.1, f32[384,1536]{1,0:T(8,128)} %input_any.1, ...), custom_call_target="tpu_custom_call" | custom-call | tf_op jit(solution)/shard_map/whole/pallas_call | solution.py:424
  75.2 1.3 %slice.20 = f32[576]{0:T(1024)} slice(f32[6144]{0:T(1024)} %bitcast.11), slice={[4608:5184]} | slice | bytes 4608 | tf_op jit(solution)/shard_map/slice | solution.py:473
  76.5 1.4 %slice_bitcast_fusion = (f32[2304]{0:T(1024)}, f32[2304]{0:T(1024)}) fusion(f32[48,128]{1,0:T(8,128)} %get-tuple-element.7), kind=kLoop, calls=%fused_computation | loop fusion | bytes 36864 | tf_op jit(solution)/shard_map/slice | solution.py:473
  77.9 2.1 %copy.15 = f32[1,512,384]{2,1,0:T(8,128)} copy(f32[1,512,384]{2,1,0:T(8,128)} %bitcast.10) | data formatting | bytes 1572864

commit v4 on v3

--- a/solution.py
+++ b/solution.py
@@ -30,6 +30,10 @@
     return pltpu.make_async_remote_copy(
         src_ref=src, dst_ref=dst, send_sem=send, recv_sem=recv, device_id=device, device_id_type=MESH
     )
+
+
+def far_first(count):
+    return sorted(range(1, count), key=lambda k: -min(k, count - k))
 
 
 def whole_kernel(
@@ -186,10 +190,8 @@
         pair_copy(n).wait_recv()
         for q in range(chips):
             z_out[n, q] = chip_sum(n, q).astype(BF16)
-        for q in range(chips):
-            @pl.when(q != chip)
-            def _():
-                along_z(n, q).start()
+        for k in far_first(chips):
+            along_z(n, lax.rem(chip + k, chips)).start()
 
     make_terms(0)
 
@@ -290,10 +292,8 @@
     conv_pair.wait_recv()
     for q in range(chips):
         cz_out[q] = (ct[2 * q + core] + cp_in[q]).astype(BF16)
-    for q in range(chips):
-        @pl.when(q != chip)
-        def _():
-            conv_z(q, chip).start()
+    for k in far_first(chips):
+        conv_z(lax.rem(chip + k, chips), chip).start()
 
     x_out[...] = jnp.zeros_like(x_out)
     for n in range(COL_BLOCKS):
@@ -317,10 +317,8 @@
     def along_v(v, landing):
         return remote(x_out.at[v], x_in.at[landing], x_send.at[v], x_recv.at[landing], (me, v))
 
-    for v in range(verts):
-        @pl.when(v != mv)
-        def _():
-            along_v(v, mv).start()
+    for k in range(1, verts):
+        along_v(lax.rem(mv + k, verts), mv).start()
 
     cx_out[...] = jnp.zeros_like(cx_out)
     cz_in[chip] = cz_out[chip]
@@ -338,10 +336,8 @@
     def conv_v(v, landing):
         return remote(cx_out.at[v // 2], cx_in.at[landing], cx_send.at[v], cx_recv.at[landing], (me, v))
 
-    for v in range(verts):
-        @pl.when(v != mv)
-        def _():
-            conv_v(v, mv).start()
+    for k in range(1, verts):
+        conv_v(lax.rem(mv + k, verts), mv).start()
     x_in[mv] = x_out[mv]
     cx_in[mv] = cx_out[mv // 2]
     for v in range(verts):

time: 80.3 us -> 80.8 us (level)
  the two profiles are of different devices: /device:TPU:248 before, /device:TPU:8 now
where the time goes in v4:
time: 80.8 us; the launch traced here: 79.7 us
  Pallas kernels  74.3 us (92%)
  local copies, waits for them, and re-layouts  4.74 us (6%)
    pallas_call x1, Pallas kernels, run_whole(): pl.pallas_call(whole_kernel, in_specs=[pl.BlockSpec(memory_space=pltpu.SM...  74.3 us
    unnamed x1, local copies, waits for them, and re-layouts  2.06 us

profile of v4, /device:TPU:8, one launch (start us, length us, event | category | flops | bytes accessed | tf_op | source)
XLA Modules:
  0.0 79.7 jit_solution(9377225918077867047)
XLA Ops:
  0.6 74.3 %whole.1 = (f32[512,384]{1,0:T(8,128)}, f32[48,128]{1,0:T(8,128)}) custom-call(s32[1,1,5]{2,1,0:T(1,128)} %mask.1, bf16[16,32,1536]{2,1,0:T(8,128)(2,1)} %gates.1, bf16[16,32,384]{2,1,0:T(8,128)(2,1)} %cells.1, f32[16,32,384]{2,1,0:T(8,128)} %grads.1, f32[384,1536]{1,0:T(8,128)} %recur.1, f32[384,1536]{1,0:T(8,128)} %input_any.1, ...), custom_call_target="tpu_custom_call" | custom-call | tf_op jit(solution)/shard_map/whole/pallas_call | solution.py:420
  75.0 1.3 %slice.20 = f32[576]{0:T(1024)} slice(f32[6144]{0:T(1024)} %bitcast.11), slice={[4608:5184]} | slice | bytes 4608 | tf_op jit(solution)/shard_map/slice | solution.py:469
  76.3 1.4 %slice_bitcast_fusion = (f32[2304]{0:T(1024)}, f32[2304]{0:T(1024)}) fusion(f32[48,128]{1,0:T(8,128)} %get-tuple-element.7), kind=kLoop, calls=%fused_computation | loop fusion | bytes 36864 | tf_op jit(solution)/shard_map/slice | solution.py:469
  77.7 2.1 %copy.15 = f32[1,512,384]{2,1,0:T(8,128)} copy(f32[1,512,384]{2,1,0:T(8,128)} %bitcast.10) | data formatting | bytes 1572864
